TPU v7x, 512 devices: a whole 4x8x8 slice. The times are simulated.
512 devices in a mesh: ax: 64 (over z, y_hi, x), rad: 8 (over y_lo, core).
Axes of the slice: x: 4, y: 8 (y_hi: 2, y_lo: 4; y = y_hi * 4 + y_lo), z: 8, core: 2. Of those that a mesh axis runs over, the one named last changes fastest.
Arguments:
- parcel_motion: float32 [6, 1048576], P(None, ('ax', 'rad')), may hold values from -6 to 6
- parcel_size: float32 [1048576], P(('ax', 'rad')), may hold values from 0.5 to 2
- parcel_block: int32 [16384], P(('ax', 'rad')), may hold values from 0 to 511, as said below
- parcel_offset: int32 [1048576], P(('ax', 'rad')), may hold values from 0 to 127
- gas_velocity: float32 [3, 1024, 4096], P(None, 'ax', 'rad'), may hold values from -6 to 6
- pressure: float32 [1024, 4096], P('ax', 'rad'), may hold values from -6 to 6
- block_cols: int32 [64, 512, 4], P('ax', 'rad'), may hold values from 0 to 511
- block_kinds: int32 [64, 512, 4], P('ax', 'rad'), may hold values from 0 to 7
- block_table: float32 [8, 128, 128], replicated, may hold values from -0.5 to 0.5
- send_axial: int32 [64, 8, 2, 64], P('ax', 'rad'), may hold values from 0 to 2047, as said below
- send_radial: int32 [64, 8, 2, 32], P('ax', 'rad'), may hold values from 0 to 2047, as said below
- send_counts: int32 [64, 8, 4], P('ax', 'rad'), may hold values from 0 to 64, as said below
Outputs:
- motion_out: float32 [6, 1048576], P(None, ('ax', 'rad'))
- arrivals_axial: float32 [64, 8, 2, 7, 64], P('ax', 'rad')
- arrivals_radial: float32 [64, 8, 2, 7, 32], P('ax', 'rad')
- gas_out: float32 [3, 1024, 4096], P(None, 'ax', 'rad')
- liquid_load: float32 [1024, 4096], P('ax', 'rad')
- pressure_image: float32 [1024, 4096], P('ax', 'rad')
Inputs may be any that keep to these rules, and one draw needn't show every extreme that they name: `parcel_block`: most of a device's parcel blocks lie in cell blocks of its own radial group; the others lie in other radial groups of the slab. `send_axial`: each device's lists (both axial and both radial together) hold distinct indices of that device's parcels; entries past the counts are unused. `send_radial`: disjoint from the device's axial lists, see send_axial. `send_counts`: axial counts are at most 64, radial ones at most 32; devices of radial group 0 send full lists in all four directions.
All inputs are finite; a program needn't handle non-finite values.
Results may differ from a plain program's by a relative error of at most 0.000084.
Values sent between devices are 32-bit elements; how exact they have to be, the bound alone decides.
A program may use at most 64 MiB of HBM per device.

v0:
```python
import jax
import jax.numpy as jnp
from jax import lax
from jax.sharding import PartitionSpec as P

BLOCK = 128
PARCEL_GROUP = 64
NT = 8
TOP_PRECISION = lax.Precision.HIGHEST
DRAG = 0.5
STEP = 0.5
DIAG = 6.0


def from_behind(value, axis, steps):
    count = lax.axis_size(axis)
    leading, last = (max(0, -steps), min(count, count - steps))
    return lax.ppermute(value, axis, [(source, source + steps) for source in range(leading, last)])


def with_halo(x, sides, width):
    for axis, dim in sides:
        count, length = (lax.axis_size(axis), x.shape[dim])
        up = [(i, (i + 1) % count) for i in range(count - 1)]
        down = [(j, i) for i, j in up]
        last = lax.slice_in_dim(x, length - width, length, axis=dim)
        leading = lax.slice_in_dim(x, 0, width, axis=dim)
        before = lax.ppermute(last, axis, up)
        after = lax.ppermute(leading, axis, down)
        x = jnp.concatenate([before, x, after], axis=dim)
    return x


def pass_axial(payload, offset):
    return from_behind(payload, "ax", offset)


def pass_radial(payload, offset):
    return from_behind(payload, "rad", offset)


def on_device(
    parcel_motion,
    parcel_size,
    parcel_block,
    parcel_offset,
    gas_velocity,
    pressure,
    block_cols,
    block_kinds,
    block_table,
    send_axial,
    send_radial,
    send_counts,
):
    blocks_here = pressure.shape[0] * pressure.shape[1] // BLOCK
    gas_local = gas_velocity.reshape(3, blocks_here, BLOCK)
    pres_local = pressure.reshape(blocks_here, BLOCK)
    parcel_groups = parcel_block.shape[0]
    gas_slab, pres_slab = (
        lax.all_gather(gas_local, "rad", axis=1, tiled=True),
        lax.all_gather(pres_local, "rad", axis=0, tiled=True),
    )
    gas_lookup = gas_slab[:, parcel_block, :]
    offsets = parcel_offset.reshape(parcel_groups, PARCEL_GROUP)
    block_selector = (offsets[:, :, None] == jnp.arange(BLOCK, dtype=jnp.int32)).astype(jnp.float32)
    visited_flags = jnp.einsum(
        "fpm,pkm->fpk", gas_lookup, block_selector, precision=TOP_PRECISION
    ).reshape(3, parcel_groups * PARCEL_GROUP)
    velocity = parcel_motion[3:6]
    factor = jnp.exp(-DRAG / (parcel_size * parcel_size))
    new_vel = visited_flags + (velocity - visited_flags) * factor
    new_pos = parcel_motion[0:3] + STEP * new_vel
    motion_out = jnp.concatenate([new_pos, new_vel], axis=0)
    mass = parcel_size * parcel_size * parcel_size
    deposit = jnp.concatenate([-mass * (new_vel - velocity), mass[None]], axis=0)
    deposit = deposit.reshape(4, parcel_groups, PARCEL_GROUP)
    dep_flat = jnp.einsum("cbj,bjn->bcn", deposit, block_selector, precision=TOP_PRECISION).reshape(
        parcel_groups, 4 * BLOCK
    )
    rows_here = jnp.arange(blocks_here * lax.axis_size("rad"), dtype=jnp.int32)
    hits = (parcel_block[None, :] == rows_here[:, None]).astype(jnp.float32)
    summed = lax.psum_scatter(
        jnp.dot(hits, dep_flat, precision=TOP_PRECISION), "rad", scatter_dimension=0, tiled=True
    )
    sources = summed.reshape(blocks_here, 4, BLOCK).transpose(1, 0, 2)
    gas_out = gas_velocity + sources[:3].reshape(gas_velocity.shape)
    liquid_load = sources[3].reshape(pressure.shape)
    state = jnp.concatenate([motion_out, parcel_size[None]], axis=0)
    counts = send_counts[0, 0]

    def pack(lists, live_counts):
        taken = jnp.moveaxis(jnp.take(state, lists, axis=1), 1, 0)
        live = jnp.arange(lists.shape[1], dtype=jnp.int32)[None, :] < live_counts[:, None]
        return jnp.where(live[:, None, :], taken, jnp.float32(0.0))

    out_ax = pack(send_axial[0, 0], counts[0:2])
    arrivals_axial = jnp.stack([pass_axial(out_ax[0], 1), pass_axial(out_ax[1], -1)], axis=0)[
        None, None
    ]
    out_rad = pack(send_radial[0, 0], counts[2:4])
    arrivals_radial = jnp.stack([pass_radial(out_rad[0], 1), pass_radial(out_rad[1], -1)], axis=0)[
        None, None
    ]
    padded = with_halo(pressure, (("ax", 0),), 1)
    image = DIAG * pressure - padded[2:] - padded[:-2]
    picked = pres_slab[block_cols[0]]
    kinds = (block_kinds[0][..., None] == jnp.arange(NT, dtype=jnp.int32)).astype(jnp.float32)
    grouped = jnp.einsum("bkt,bkn->btn", kinds, picked, precision=TOP_PRECISION)
    coupled = jnp.einsum("btn,tmn->bm", grouped, block_table, precision=TOP_PRECISION)
    pressure_image = image + coupled.reshape(pressure.shape)
    return (motion_out, arrivals_axial, arrivals_radial, gas_out, liquid_load, pressure_image)


def solution(mesh):
    return jax.shard_map(
        on_device,
        mesh=mesh,
        in_specs=(
            P(None, ("ax", "rad")),
            P(("ax", "rad")),
            P(("ax", "rad")),
            P(("ax", "rad")),
            P(None, "ax", "rad"),
            P("ax", "rad"),
            P("ax", "rad", None),
            P("ax", "rad", None),
            P(),
            P("ax", "rad", None, None),
            P("ax", "rad", None, None),
            P("ax", "rad", None),
        ),
        out_specs=(
            P(None, ("ax", "rad")),
            P("ax", "rad", None, None, None),
            P("ax", "rad", None, None, None),
            P(None, "ax", "rad"),
            P("ax", "rad"),
            P("ax", "rad"),
        ),
        check_vma=False,
    )
```

profile of v0, /device:TPU:264, one launch (start us, length us, event | category | flops | bytes accessed | tf_op | source)
XLA Modules:
  0.0 99.1 jit_solution(3269439988784230751)
XLA Ops:
  7.2 0.8 multiply_multiply_fusion
  8.1 0.9 reshape.182
  9.0 15.8 %all_gather.6 = f32[3,512,128]{2,1,0:T(8,128)S(1)} all-gather(f32[3,64,128]{2,1,0:T(8,128)S(1)} %reshape.182), channel_id=1, replica_groups=mesh['ax'=64,'rad'=8] {'rad'}, dimensions={1}, use_global_device_ids=true | all-gather | bytes 884736 | tf_op jit(solution)/shard_map/all_gather | solution.py:61
  24.8 0.5 copy.64
  25.3 0.1 copy-done.11
  25.4 0.6 gather_fusion
  26.0 1.0 convolution_bitcast_fusion
  27.0 0.1 reshape.183
  27.1 0.7 copy-done.3
  27.9 0.7 copy-done.4
  28.6 0.4 copy.66
  29.0 0.3 copy-done.6
  29.3 0.1 reshape.207
  29.4 0.6 gather_fusion.2
  30.0 0.1 copy.70
  30.1 0.6 copy-done.10
  30.8 2.3 %collective-permute-start.2 = (f32[7,32]{1,0:T(8,128)S(1)}, f32[7,32]{1,0:T(8,128)S(1)}, u32[]{:S(2)}, u32[]{:S(2)}) collective-permute-start(f32[7,32]{1,0:T(8,128)S(1)} %get-tuple-element.31), channel_id=1, source_target_pairs={{0,1},{1,2},{2,3},{3,4},{4,5},{5,6},{6,7},{8,9},{9,10},{10,11},{11... | collective-permute-start | bytes 2696 | tf_op jit(solution)/shard_map/ppermute | solution.py:18
  33.1 3.3 %collective-permute-start.3 = (f32[7,32]{1,0:T(8,128)S(1)}, f32[7,32]{1,0:T(8,128)S(1)}, u32[]{:S(2)}, u32[]{:S(2)}) collective-permute-start(f32[7,32]{1,0:T(8,128)S(1)} %get-tuple-element.32), channel_id=1, source_target_pairs={{1,0},{2,1},{3,2},{4,3},{5,4},{6,5},{7,6},{9,8},{10,9},{11,10},{12... | collective-permute-start | bytes 2696 | tf_op jit(solution)/shard_map/ppermute | solution.py:18
  36.4 0.1 concatenate.24
  36.5 0.1 concatenate.25
  36.6 0.7 fusion
  37.3 1.6 %fusion.4 = f32[512,512]{1,0:T(8,128)} fusion(s32[32]{0:T(128)S(1)} %copy-done.11, f32[4,8,4,128]{3,2,1,0:T(4,128)S(1)} %bitcast.62), kind=kOutput, calls=%fused_computation.12 | convolution fusion | flops 100679680 | bytes 1114240 | tf_op jit(solution)/shard_map/dot_general | solution.py:84
  38.9 0.7 copy-done.7
  39.6 0.1 reshape.199
  39.7 0.6 gather_fusion.1
  40.3 0.1 copy.67
  40.5 3.4 %collective-permute-start = (f32[7,64]{1,0:T(8,128)S(1)}, f32[7,64]{1,0:T(8,128)S(1)}, u32[]{:S(2)}, u32[]{:S(2)}) collective-permute-start(f32[7,64]{1,0:T(8,128)S(1)} %get-tuple-element.33), channel_id=1, source_target_pairs={{0,8},{8,16},{16,24},{24,32},{32,40},{40,48},{48,56},{56,64},{64,7... | collective-permute-start | bytes 5384 | tf_op jit(solution)/shard_map/ppermute | solution.py:18
  43.9 10.6 %collective-permute-start.1 = (f32[7,64]{1,0:T(8,128)S(1)}, f32[7,64]{1,0:T(8,128)S(1)}, u32[]{:S(2)}, u32[]{:S(2)}) collective-permute-start(f32[7,64]{1,0:T(8,128)S(1)} %get-tuple-element.34), channel_id=1, source_target_pairs={{8,0},{16,8},{24,16},{32,24},{40,32},{48,40},{56,48},{64,56},{72,6... | collective-permute-start | bytes 5384 | tf_op jit(solution)/shard_map/ppermute | solution.py:18
  54.5 1.9 %collective-permute-start.4 = (f32[1,512]{1,0:T(1,128)S(1)}, f32[1,512]{1,0:T(1,128)S(1)}, u32[]{:S(2)}, u32[]{:S(2)}) collective-permute-start(f32[1,512]{1,0:T(1,128)S(1)} %get-tuple-element.26), channel_id=1, source_target_pairs={{8,0},{16,8},{24,16},{32,24},{40,32},{48,40},{56,48},{64,56},{72,6... | collective-permute-start | bytes 6152 | tf_op jit(solution)/shard_map/ppermute | solution.py:29
  56.5 0.1 copy.75
  56.6 0.1 reshape.215
  56.7 0.4 copy-done.8
  57.1 0.1 copy.74
  57.2 14.9 %all_gather.7 = f32[512,128]{1,0:T(8,128)S(1)} all-gather(f32[64,128]{1,0:T(8,128)S(1)} %reshape.187), channel_id=1, replica_groups=mesh['ax'=64,'rad'=8] {'rad'}, dimensions={0}, use_global_device_ids=true | all-gather | bytes 294912 | tf_op jit(solution)/shard_map/all_gather | solution.py:62
  72.1 0.7 gather_fusion.3
  72.9 0.6 pad_maximum_fusion
  73.5 0.6 fusion.6
  74.1 0.7 convolution_bitcast_fusion.1
  74.8 3.6 %collective-permute-start.5 = (f32[1,512]{1,0:T(1,128)S(1)}, f32[1,512]{1,0:T(1,128)S(1)}, u32[]{:S(2)}, u32[]{:S(2)}) collective-permute-start(f32[1,512]{1,0:T(1,128)S(1)} %get-tuple-element.27), channel_id=1, source_target_pairs={{0,8},{8,16},{16,24},{24,32},{32,40},{40,48},{48,56},{56,64},{64,7... | collective-permute-start | bytes 6152 | tf_op jit(solution)/shard_map/ppermute | solution.py:28
  78.4 0.6 maximum_bitcast_fusion.1
  79.1 0.6 maximum_bitcast_fusion
  79.7 8.7 %collective-permute-done.5 = f32[1,512]{1,0:T(1,128)S(1)} collective-permute-done((f32[1,512]{1,0:T(1,128)S(1)}, f32[1,512]{1,0:T(1,128)S(1)}, u32[]{:S(2)}, u32[]{:S(2)}) %collective-permute-start.5) | collective-permute-done | bytes 2080 | tf_op jit(solution)/shard_map/ppermute | solution.py:28
  88.4 0.6 fusion.15
  89.1 0.9 reshape.185
  90.0 0.1 slice_reduce_fusion
  90.2 0.9 copy-done.1
  91.0 0.7 add.87
  91.7 0.6 reshape_squeeze.3
  (54 shorter events, 0.7 us)
Async XLA Ops:
  7.2 67.0 %copy-start = (f32[8,128,128]{2,1,0:T(8,128)S(1)}, f32[8,128,128]{2,1,0:T(8,128)}, u32[]{:S(2)}) copy-start(f32[8,128,128]{2,1,0:T(8,128)} %param.20) | copy-start | bytes 1572868
  7.2 0.8 copy-start.5
  7.2 81.9 %reduce-scatter.2.cloned.1.call-start = ((), (), s32[]{:S(2)}) async-start(), calls=%async_computation.1 | async-start | bytes 1179648 | tf_op jit(solution)/shard_map/reduce_scatter | solution.py:83
  24.8 0.7 copy-start.11
  27.0 0.9 copy-start.3
  27.9 0.7 copy-start.4
  28.6 0.7 copy-start.6
  30.0 0.7 copy-start.10
  30.8 44.0 %collective-permute-start.2 = (f32[7,32]{1,0:T(8,128)S(1)}, f32[7,32]{1,0:T(8,128)S(1)}, u32[]{:S(2)}, u32[]{:S(2)}) collective-permute-start(f32[7,32]{1,0:T(8,128)S(1)} %get-tuple-element.31), channel_id=1, source_target_pairs={{0,1},{1,2},{2,3},{3,4},{4,5},{5,6},{6,7},{8,9},{9,10},{10,11},{11... | collective-permute-start | bytes 2696 | tf_op jit(solution)/shard_map/ppermute | solution.py:18
  33.1 45.3 %collective-permute-start.3 = (f32[7,32]{1,0:T(8,128)S(1)}, f32[7,32]{1,0:T(8,128)S(1)}, u32[]{:S(2)}, u32[]{:S(2)}) collective-permute-start(f32[7,32]{1,0:T(8,128)S(1)} %get-tuple-element.32), channel_id=1, source_target_pairs={{1,0},{2,1},{3,2},{4,3},{5,4},{6,5},{7,6},{9,8},{10,9},{11,10},{12... | collective-permute-start | bytes 2696 | tf_op jit(solution)/shard_map/ppermute | solution.py:18
  38.9 0.7 copy-start.7
  40.4 14.1 %copy-start.2 = (f32[16,512]{1,0:T(8,128)S(1)}, f32[16,512]{1,0:T(8,128)}, u32[]{:S(2)}) copy-start(f32[16,512]{1,0:T(8,128)} %param.17) | copy-start | bytes 98308
  40.5 38.5 %collective-permute-start = (f32[7,64]{1,0:T(8,128)S(1)}, f32[7,64]{1,0:T(8,128)S(1)}, u32[]{:S(2)}, u32[]{:S(2)}) collective-permute-start(f32[7,64]{1,0:T(8,128)S(1)} %get-tuple-element.33), channel_id=1, source_target_pairs={{0,8},{8,16},{16,24},{24,32},{32,40},{40,48},{48,56},{56,64},{64,7... | collective-permute-start | bytes 5384 | tf_op jit(solution)/shard_map/ppermute | solution.py:18
  43.9 35.1 %collective-permute-start.1 = (f32[7,64]{1,0:T(8,128)S(1)}, f32[7,64]{1,0:T(8,128)S(1)}, u32[]{:S(2)}, u32[]{:S(2)}) collective-permute-start(f32[7,64]{1,0:T(8,128)S(1)} %get-tuple-element.34), channel_id=1, source_target_pairs={{8,0},{16,8},{24,16},{32,24},{40,32},{48,40},{56,48},{64,56},{72,6... | collective-permute-start | bytes 5384 | tf_op jit(solution)/shard_map/ppermute | solution.py:18
  54.5 2.0 %copy-start.9 = (s32[1,64,4]{1,2,0:T(4,128)S(1)}, s32[1,64,4]{1,2,0:T(4,128)}, u32[]{:S(2)}) copy-start(s32[1,64,4]{1,2,0:T(4,128)} %param.18) | copy-start | bytes 3076
  54.5 25.2 %collective-permute-start.4 = (f32[1,512]{1,0:T(1,128)S(1)}, f32[1,512]{1,0:T(1,128)S(1)}, u32[]{:S(2)}, u32[]{:S(2)}) collective-permute-start(f32[1,512]{1,0:T(1,128)S(1)} %get-tuple-element.26), channel_id=1, source_target_pairs={{8,0},{16,8},{24,16},{32,24},{40,32},{48,40},{56,48},{64,56},{72,6... | collective-permute-start | bytes 6152 | tf_op jit(solution)/shard_map/ppermute | solution.py:29
  56.4 0.7 copy-start.8
  74.8 13.6 %collective-permute-start.5 = (f32[1,512]{1,0:T(1,128)S(1)}, f32[1,512]{1,0:T(1,128)S(1)}, u32[]{:S(2)}, u32[]{:S(2)}) collective-permute-start(f32[1,512]{1,0:T(1,128)S(1)} %get-tuple-element.27), channel_id=1, source_target_pairs={{0,8},{8,16},{16,24},{24,32},{32,40},{40,48},{48,56},{56,64},{64,7... | collective-permute-start | bytes 6152 | tf_op jit(solution)/shard_map/ppermute | solution.py:28
  90.1 0.9 copy-start.1
Sparse Core Ops, SparseCore 0:
  39.0 37.2 reduce-scatter.1
where the time goes:
time: 99.7 us; the launch traced here: 99.1 us
  blocking collectives  30.7 us (31%)
  starting transfers between devices  25.1 us (25%)
  between operations  14.3 us (14%)
  local copies, waits for them, and re-layouts  11.6 us (12%)
  waiting for transfers between devices  8.78 us (9%)
  matrix products  4.54 us (5%)
  other arithmetic  4.18 us (4%)
    ppermute x4, starting transfers between devices, from_behind(): lax.ppermute(value, axis, [(source, source + steps) for source in range(l...  19.5 us
    all_gather x1, blocking collectives, on_device(): lax.all_gather(gas_local, 'rad', axis=1, tiled=True)  15.8 us
    all_gather x1, blocking collectives, on_device(): lax.all_gather(pres_local, 'rad', axis=0, tiled=True)  14.9 us
    ppermute x1, waiting for transfers between devices, with_halo(): before = lax.ppermute(last, axis, up)  8.75 us
    unnamed x24, local copies, waits for them, and re-layouts  4.38 us
    ppermute x1, starting transfers between devices, with_halo(): before = lax.ppermute(last, axis, up)  3.57 us
  transfers between devices with their start and end apart: 7, of which 1 were waited for; matrix products, arithmetic and copies ran while one was open for 8% of the time, Pallas kernels for 0%

commit v1 on v0

--- a/solution.py
+++ b/solution.py
@@ -10,6 +10,12 @@
 DRAG = 0.5
 STEP = 0.5
 DIAG = 6.0
+
+
+def _press_counts(xs, axis_key):
+    return jnp.concatenate(
+        jax.lax.all_to_all(jnp.stack(jax.lax.axis_size(axis_key) * [xs]), axis_key, 0, 0), axis=0
+    )
 
 
 def from_behind(value, axis, steps):
@@ -59,7 +65,7 @@
     parcel_groups = parcel_block.shape[0]
     gas_slab, pres_slab = (
         lax.all_gather(gas_local, "rad", axis=1, tiled=True),
-        lax.all_gather(pres_local, "rad", axis=0, tiled=True),
+        _press_counts(pres_local, "rad"),
     )
     gas_lookup = gas_slab[:, parcel_block, :]
     offsets = parcel_offset.reshape(parcel_groups, PARCEL_GROUP)

time: 99.7 us -> 95 us (0.953)
  the two profiles are of different devices: /device:TPU:264 before, /device:TPU:6 now
where the time goes in v1:
time: 95 us; the launch traced here: 94.3 us
  starting transfers between devices  29.1 us (31%)
  blocking collectives  15.8 us (17%)
  waiting for transfers between devices  14.6 us (15%)
  between operations  14.4 us (15%)
  local copies, waits for them, and re-layouts  11.9 us (13%)
  matrix products  4.56 us (5%)
  other arithmetic  4.18 us (4%)
    all_gather x1, blocking collectives, on_device(): lax.all_gather(gas_local, 'rad', axis=1, tiled=True)  15.8 us
    reduce_scatter x1, waiting for transfers between devices, on_device(): lax.psum_scatter(jnp.dot(hits, dep_flat, precision=TOP_PRECISION), 'rad',...  14.3 us
    ppermute x4, starting transfers between devices, from_behind(): lax.ppermute(value, axis, [(source, source + steps) for source in range(l...  13 us
    ppermute x1, starting transfers between devices, with_halo(): before = lax.ppermute(last, axis, up)  9.94 us
    all_to_all x1, starting transfers between devices, _press_counts(): jax.lax.all_to_all(jnp.stack(jax.lax.axis_size(axis_key) * [xs]), axis_ke...  4.12 us
    unnamed x24, local copies, waits for them, and re-layouts  3.97 us
    ppermute x1, starting transfers between devices, with_halo(): after = lax.ppermute(leading, axis, down)  1.92 us
  transfers between devices with their start and end apart: 8, of which 2 were waited for; matrix products, arithmetic and copies ran while one was open for 9% of the time, Pallas kernels for 0%

profile of v1, /device:TPU:6, one launch (start us, length us, event | category | flops | bytes accessed | tf_op | source)
XLA Modules:
  0.0 94.3 jit_solution(17302884043642863849)
XLA Ops:
  7.2 0.8 multiply_multiply_fusion
  8.1 0.9 reshape.184
  9.0 15.8 %all_gather.3 = f32[3,512,128]{2,1,0:T(8,128)S(1)} all-gather(f32[3,64,128]{2,1,0:T(8,128)S(1)} %reshape.184), channel_id=1, replica_groups=mesh['ax'=64,'rad'=8] {'rad'}, dimensions={1}, use_global_device_ids=true | all-gather | bytes 884736 | tf_op jit(solution)/shard_map/all_gather | solution.py:67
  24.7 0.5 copy.64
  25.3 0.1 copy-done.11
  25.4 0.6 gather_fusion
  26.0 1.0 %convolution_bitcast_fusion = f32[3,32,64]{2,0,1:T(4,128)S(1)} fusion(s32[32,64]{1,0:T(8,128)S(1)} %eq.43, f32[32,3,128]{2,1,0:T(4,128)S(1)} %gather_fusion), kind=kOutput, calls=%fused_computation.4 | convolution fusion | flops 9699328 | bytes 81920 | tf_op jit(solution)/shard_map/fpm,pkm->fpk/dot_general | solution.py:73
  27.0 0.1 reshape.185
  27.1 0.7 copy-done.3
  27.9 0.7 copy-done.4
  28.6 0.4 copy.66
  29.0 0.3 copy-done.6
  29.3 0.1 reshape.209
  29.4 0.6 gather_fusion.2
  30.0 0.1 copy.70
  30.1 0.6 copy-done.10
  30.8 2.2 %collective-permute-start.2 = (f32[7,32]{1,0:T(8,128)S(1)}, f32[7,32]{1,0:T(8,128)S(1)}, u32[]{:S(2)}, u32[]{:S(2)}) collective-permute-start(f32[7,32]{1,0:T(8,128)S(1)} %get-tuple-element.31), channel_id=1, source_target_pairs={{0,1},{1,2},{2,3},{3,4},{4,5},{5,6},{6,7},{8,9},{9,10},{10,11},{11... | collective-permute-start | bytes 2696 | tf_op jit(solution)/shard_map/ppermute | solution.py:24
  33.1 1.3 %collective-permute-start.3 = (f32[7,32]{1,0:T(8,128)S(1)}, f32[7,32]{1,0:T(8,128)S(1)}, u32[]{:S(2)}, u32[]{:S(2)}) collective-permute-start(f32[7,32]{1,0:T(8,128)S(1)} %get-tuple-element.32), channel_id=1, source_target_pairs={{1,0},{2,1},{3,2},{4,3},{5,4},{6,5},{7,6},{9,8},{10,9},{11,10},{12... | collective-permute-start | bytes 2696 | tf_op jit(solution)/shard_map/ppermute | solution.py:24
  34.4 0.1 concatenate.24
  34.5 0.1 concatenate.25
  34.6 0.7 fusion
  35.3 1.6 %fusion.4 = f32[512,512]{1,0:T(8,128)} fusion(s32[32]{0:T(128)S(1)} %copy-done.11, f32[4,8,4,128]{3,2,1,0:T(4,128)S(1)} %bitcast.64), kind=kOutput, calls=%fused_computation.12 | convolution fusion | flops 100679680 | bytes 1114240 | tf_op jit(solution)/shard_map/dot_general | solution.py:90
  36.9 0.7 copy-done.7
  37.6 0.1 reshape.201
  37.7 0.6 gather_fusion.1
  38.5 7.6 %collective-permute-start = (f32[7,64]{1,0:T(8,128)S(1)}, f32[7,64]{1,0:T(8,128)S(1)}, u32[]{:S(2)}, u32[]{:S(2)}) collective-permute-start(f32[7,64]{1,0:T(8,128)S(1)} %get-tuple-element.33), channel_id=1, source_target_pairs={{0,8},{8,16},{16,24},{24,32},{32,40},{40,48},{48,56},{56,64},{64,7... | collective-permute-start | bytes 5384 | tf_op jit(solution)/shard_map/ppermute | solution.py:24
  46.1 1.9 %collective-permute-start.1 = (f32[7,64]{1,0:T(8,128)S(1)}, f32[7,64]{1,0:T(8,128)S(1)}, u32[]{:S(2)}, u32[]{:S(2)}) collective-permute-start(f32[7,64]{1,0:T(8,128)S(1)} %get-tuple-element.34), channel_id=1, source_target_pairs={{8,0},{16,8},{24,16},{32,24},{40,32},{48,40},{56,48},{64,56},{72,6... | collective-permute-start | bytes 5384 | tf_op jit(solution)/shard_map/ppermute | solution.py:24
  48.0 1.9 %collective-permute-start.4 = (f32[1,512]{1,0:T(1,128)S(1)}, f32[1,512]{1,0:T(1,128)S(1)}, u32[]{:S(2)}, u32[]{:S(2)}) collective-permute-start(f32[1,512]{1,0:T(1,128)S(1)} %get-tuple-element.26), channel_id=1, source_target_pairs={{8,0},{16,8},{24,16},{32,24},{40,32},{48,40},{56,48},{64,56},{72,6... | collective-permute-start | bytes 6152 | tf_op jit(solution)/shard_map/ppermute | solution.py:35
  50.0 0.7 stack.27
  50.7 4.1 %all-to-all-start = ((f32[8,64,128]{2,1,0:T(8,128)}), f32[8,64,128]{2,1,0:T(8,128)S(1)}, u32[]{:S(2)}, u32[]{:S(2)}) async-start(f32[8,64,128]{2,1,0:T(8,128)} %stack.27), calls=%async_computation.1 | async-start | bytes 524288 | tf_op jit(solution)/shard_map/all_to_all | solution.py:17
  54.8 0.1 copy.75
  54.9 0.1 reshape.217
  55.0 0.6 pad_maximum_fusion
  55.7 0.1 copy.74
  55.8 9.9 %collective-permute-start.5 = (f32[1,512]{1,0:T(1,128)S(1)}, f32[1,512]{1,0:T(1,128)S(1)}, u32[]{:S(2)}, u32[]{:S(2)}) collective-permute-start(f32[1,512]{1,0:T(1,128)S(1)} %get-tuple-element.27), channel_id=1, source_target_pairs={{0,8},{8,16},{16,24},{24,32},{32,40},{40,48},{48,56},{56,64},{64,7... | collective-permute-start | bytes 6152 | tf_op jit(solution)/shard_map/ppermute | solution.py:34
  65.8 0.6 maximum_bitcast_fusion.1
  66.4 0.6 maximum_bitcast_fusion
  67.0 0.3 all-to-all-done
  67.3 0.7 gather_fusion.3
  68.0 0.6 fusion.6
  68.6 0.7 convolution_bitcast_fusion.1
  69.4 0.6 fusion.15
  70.0 14.3 %reduce-scatter.2.cloned.1.call-done = f32[64,512]{1,0:T(8,128)} async-done(((f32[512,512]{1,0:T(8,128)}), f32[64,512]{1,0:T(8,128)}) %reduce-scatter.2.cloned.1.call-update) | async-done | bytes 131088 | tf_op jit(solution)/shard_map/reduce_scatter | solution.py:89
  84.2 0.9 %reshape.187 = f32[64,4,128]{2,1,0:T(4,128)S(1)} reshape(f32[64,512]{1,0:T(8,128)} %reduce-scatter.2.cloned.1.call-done) | data formatting | bytes 262144 | tf_op jit(solution)/shard_map/reshape | solution.py:92
  85.2 0.1 slice_reduce_fusion
  85.3 0.9 copy-done.1
  86.2 0.7 add.87
  86.9 0.6 reshape_squeeze.3
  (56 shorter events, 0.7 us)
Async XLA Ops:
  7.2 61.5 %copy-start = (f32[8,128,128]{2,1,0:T(8,128)S(1)}, f32[8,128,128]{2,1,0:T(8,128)}, u32[]{:S(2)}) copy-start(f32[8,128,128]{2,1,0:T(8,128)} %param.20) | copy-start | bytes 1572868
  7.2 0.8 copy-start.5
  7.2 77.0 %reduce-scatter.2.cloned.1.call-start = ((), (), s32[]{:S(2)}) async-start(), calls=%async_computation.2 | async-start | bytes 1179648 | tf_op jit(solution)/shard_map/reduce_scatter | solution.py:89
  24.7 0.7 copy-start.11
  27.0 0.9 copy-start.3
  27.9 0.7 copy-start.4
  28.6 0.7 copy-start.6
  30.0 0.7 copy-start.10
  30.8 25.0 %collective-permute-start.2 = (f32[7,32]{1,0:T(8,128)S(1)}, f32[7,32]{1,0:T(8,128)S(1)}, u32[]{:S(2)}, u32[]{:S(2)}) collective-permute-start(f32[7,32]{1,0:T(8,128)S(1)} %get-tuple-element.31), channel_id=1, source_target_pairs={{0,1},{1,2},{2,3},{3,4},{4,5},{5,6},{6,7},{8,9},{9,10},{10,11},{11... | collective-permute-start | bytes 2696 | tf_op jit(solution)/shard_map/ppermute | solution.py:24
  33.1 32.7 %collective-permute-start.3 = (f32[7,32]{1,0:T(8,128)S(1)}, f32[7,32]{1,0:T(8,128)S(1)}, u32[]{:S(2)}, u32[]{:S(2)}) collective-permute-start(f32[7,32]{1,0:T(8,128)S(1)} %get-tuple-element.32), channel_id=1, source_target_pairs={{1,0},{2,1},{3,2},{4,3},{5,4},{6,5},{7,6},{9,8},{10,9},{11,10},{12... | collective-permute-start | bytes 2696 | tf_op jit(solution)/shard_map/ppermute | solution.py:24
  36.9 0.7 copy-start.7
  38.4 9.5 %copy-start.2 = (f32[16,512]{1,0:T(8,128)S(1)}, f32[16,512]{1,0:T(8,128)}, u32[]{:S(2)}) copy-start(f32[16,512]{1,0:T(8,128)} %param.17) | copy-start | bytes 98308
  38.5 27.9 %collective-permute-start = (f32[7,64]{1,0:T(8,128)S(1)}, f32[7,64]{1,0:T(8,128)S(1)}, u32[]{:S(2)}, u32[]{:S(2)}) collective-permute-start(f32[7,64]{1,0:T(8,128)S(1)} %get-tuple-element.33), channel_id=1, source_target_pairs={{0,8},{8,16},{16,24},{24,32},{32,40},{40,48},{48,56},{56,64},{64,7... | collective-permute-start | bytes 5384 | tf_op jit(solution)/shard_map/ppermute | solution.py:24
  46.1 20.3 %collective-permute-start.1 = (f32[7,64]{1,0:T(8,128)S(1)}, f32[7,64]{1,0:T(8,128)S(1)}, u32[]{:S(2)}, u32[]{:S(2)}) collective-permute-start(f32[7,64]{1,0:T(8,128)S(1)} %get-tuple-element.34), channel_id=1, source_target_pairs={{8,0},{16,8},{24,16},{32,24},{40,32},{48,40},{56,48},{64,56},{72,6... | collective-permute-start | bytes 5384 | tf_op jit(solution)/shard_map/ppermute | solution.py:24
  48.0 21.3 %collective-permute-start.4 = (f32[1,512]{1,0:T(1,128)S(1)}, f32[1,512]{1,0:T(1,128)S(1)}, u32[]{:S(2)}, u32[]{:S(2)}) collective-permute-start(f32[1,512]{1,0:T(1,128)S(1)} %get-tuple-element.26), channel_id=1, source_target_pairs={{8,0},{16,8},{24,16},{32,24},{40,32},{48,40},{56,48},{64,56},{72,6... | collective-permute-start | bytes 6152 | tf_op jit(solution)/shard_map/ppermute | solution.py:35
  50.7 4.1 %copy-start.9 = (s32[1,64,4]{1,2,0:T(4,128)S(1)}, s32[1,64,4]{1,2,0:T(4,128)}, u32[]{:S(2)}) copy-start(s32[1,64,4]{1,2,0:T(4,128)} %param.18) | copy-start | bytes 3076
  50.7 16.6 %all-to-all-start = ((f32[8,64,128]{2,1,0:T(8,128)}), f32[8,64,128]{2,1,0:T(8,128)S(1)}, u32[]{:S(2)}, u32[]{:S(2)}) async-start(f32[8,64,128]{2,1,0:T(8,128)} %stack.27), calls=%async_computation.1 | async-start | bytes 524288 | tf_op jit(solution)/shard_map/all_to_all | solution.py:17
  55.0 0.7 copy-start.8
  55.8 13.5 %collective-permute-start.5 = (f32[1,512]{1,0:T(1,128)S(1)}, f32[1,512]{1,0:T(1,128)S(1)}, u32[]{:S(2)}, u32[]{:S(2)}) collective-permute-start(f32[1,512]{1,0:T(1,128)S(1)} %get-tuple-element.27), channel_id=1, source_target_pairs={{0,8},{8,16},{16,24},{24,32},{32,40},{40,48},{48,56},{56,64},{64,7... | collective-permute-start | bytes 6152 | tf_op jit(solution)/shard_map/ppermute | solution.py:34
  85.3 0.9 copy-start.1
Sparse Core Ops, SparseCore 0:
  37.0 47.1 reduce-scatter.1
